TPU v7x, 32 devices: a whole 2x2x4 slice. The times are simulated.
32 devices in a mesh: row: 4 (over z), col: 8 (over y, x, core).
Axes of the slice: x: 2, y: 2, z: 4, core: 2. Of those that a mesh axis runs over, the one named last changes fastest.
Arguments:
- velocity: bfloat16 [3, 8, 2048, 2048], P(None, 'col', 'row'), may hold values from -6 to 6
- vorticity: bfloat16 [3, 8, 2048, 2048], P(None, 'col', 'row'), may hold values from -6 to 6
- eddy_state: bfloat16 [8, 64, 3072], P('col', 'row'), may hold values from -0.359375 to 0.359375
- eddy_rate: bfloat16 [8, 64], P('col', 'row'), may hold values from 8 to 64
- block_owner: int32 [8, 4, 64, 1], P('col', 'row'), may hold values from 0 to 3; in each aligned block of 64 rows (0 to 63, 64 to 127, ..., all dimensions but the last counted through in order) at most 32 rows name the same one
- block_slot: int32 [8, 4, 64], P('col', 'row'), may hold values from 0 to 15
Outputs:
- spectral: float32 [3, 8, 1638400], P(None, None, ('row', 'col'))
Inputs may be any that keep to these rules, and one draw needn't show every extreme that they name: `block_owner`: among the 64 blocks of one DNS device, at most 32 have the same owner.
All inputs are finite; a program needn't handle non-finite values.
Results may differ from a plain program's by a relative error of at most 0.013.
Values may be sent and summed in bfloat16 or wider, within the bound.
A program may use at most 128 MiB of HBM per device.

v0:
```python
import math

import jax
import jax.numpy as jnp
import numpy as np
from jax import lax
from jax.experimental import pallas as pl
from jax.experimental.pallas import tpu as pltpu
from jax.sharding import PartitionSpec as P

NX = 2048
NY = 2048
KXM = 640
KYM = 1280
RATIO = 4
BY = 8
BX = 128
S = 16
BLKV = 3072


section_step = 0.5
viscous_step = 0.15
vertical_step = 0.5


def padded_2(cells, sides, width):
    for axis, dim in sides:
        count = lax.axis_size(axis)
        head = lax.slice_in_dim(cells, 0, width, axis=dim)
        tail = lax.slice_in_dim(cells, cells.shape[dim] - width, cells.shape[dim], axis=dim)
        cells = jnp.concatenate(
            [
                lax.ppermute(tail, axis, [(i, (i + 1) % count) for i in range(count)]),
                cells,
                lax.ppermute(head, axis, [((i + 1) % count, i) for i in range(count)]),
            ],
            axis=dim,
        )
    return cells


def gauss_value(position, ratio):
    spread = 4.0 * ratio * ratio
    taps = jnp.arange(5 * ratio).astype(jnp.float32)
    shifted = taps - 2.0 * ratio - (ratio - 1) / 2.0
    total = jnp.sum(jnp.exp(-shifted * shifted / (2.0 * spread)))
    moved = position - 2.0 * ratio - (ratio - 1) / 2.0
    return jnp.exp(-moved * moved / (2.0 * spread)) / total


def x_weights(points, coarse, ratio):
    fine = jnp.arange(points, dtype=jnp.int32)[:, None]
    cells = jnp.arange(coarse, dtype=jnp.int32)[None, :]
    offset = jnp.mod(fine - ratio * cells + 2 * ratio, points)
    value = gauss_value(offset.astype(jnp.float32), ratio)
    return jnp.where(offset < 5 * ratio, value, 0.0).astype(jnp.bfloat16)


def y_weights(coarse, padded, ratio):
    cells = jnp.arange(coarse, dtype=jnp.int32)[:, None]
    fine = jnp.arange(padded, dtype=jnp.int32)[None, :]
    offset = fine - ratio * cells
    value = gauss_value(offset.astype(jnp.float32), ratio)
    return jnp.where((offset >= 0) & (offset < 5 * ratio), value, 0.0).astype(jnp.bfloat16)


def x_table(points, kept):
    fine = jnp.arange(points, dtype=jnp.int32)[:, None]
    column = jnp.arange(2 * kept, dtype=jnp.int32)[None, :]
    phase = jnp.mod(column // 2 * fine, points).astype(jnp.float32) * (2.0 * math.pi / points)
    value = jnp.where(column % 2 == 0, jnp.cos(phase), -jnp.sin(phase))
    return (value / math.sqrt(points)).astype(jnp.bfloat16)


def y_tables(points, kept, first, count):
    fine = jnp.arange(points, dtype=jnp.int32)[:, None]
    wave = jnp.arange(count, dtype=jnp.int32)[None, :] + (first - kept // 2)
    phase = jnp.mod(wave * fine, points).astype(jnp.float32) * (2.0 * math.pi / points)
    scale = 1.0 / math.sqrt(points)
    return (
        (jnp.cos(phase) * scale).astype(jnp.bfloat16),
        (jnp.sin(phase) * scale).astype(jnp.bfloat16),
    )


def vertical_inverse(planes):
    index = jnp.arange(planes)
    ends = (index == 0) | (index == planes - 1)
    diagonal = jnp.where(ends, 1.0 + vertical_step, 1.0 + 2.0 * vertical_step).astype(jnp.float32)
    lower = jnp.where(index == 0, 0.0, -vertical_step).astype(jnp.float32)
    upper = jnp.where(index == planes - 1, 0.0, -vertical_step).astype(jnp.float32)
    return lax.linalg.tridiagonal_solve(lower, diagonal, upper, jnp.eye(planes, dtype=jnp.float32))


def damping(x_wave, y_wave, points_x, points_y):
    angle_x = x_wave.astype(jnp.float32) * (2.0 * math.pi / points_x)
    angle_y = y_wave.astype(jnp.float32) * (2.0 * math.pi / points_y)
    total = (
        angle_y[:, None, None] * angle_y[:, None, None]
        + angle_x[None, None, :] * angle_x[None, None, :]
    )
    return jnp.broadcast_to(jnp.exp(-viscous_step * total), (y_wave.shape[0], 2, x_wave.shape[0]))


def along_y(piece):
    items, width, length = piece.shape
    half = width // 2
    split = piece.reshape(items, half, 2, length)
    real_in = split[:, :, 0, :]
    imag_in = split[:, :, 1, :]
    block = 256
    outputs = []
    for first in range(0, KYM, block):
        cosine, sine = y_tables(length, KYM, first, block)
        real_out = jnp.einsum(
            "kin,nj->kji", real_in, cosine, preferred_element_type=jnp.float32
        ) + jnp.einsum("kin,nj->kji", imag_in, sine, preferred_element_type=jnp.float32)
        imag_out = jnp.einsum(
            "kin,nj->kji", imag_in, cosine, preferred_element_type=jnp.float32
        ) - jnp.einsum("kin,nj->kji", real_in, sine, preferred_element_type=jnp.float32)
        outputs.append(jnp.concatenate([real_out, imag_out], axis=2))
    return jnp.concatenate(outputs, axis=1).astype(jnp.bfloat16)


def generic_device(velocity, vorticity, eddy_state, eddy_rate, block_owner, block_slot):
    components, depth, rows, points = velocity.shape
    coarse_rows = rows // RATIO
    coarse_cols = points // RATIO
    xweights = x_weights(points, coarse_cols, RATIO)
    local = jnp.einsum(
        "czyn,nx->czyx", velocity, xweights, preferred_element_type=jnp.float32
    ).astype(jnp.bfloat16)
    along = padded_2(local, (("row", 2),), 2 * RATIO)
    yweights = y_weights(coarse_rows, rows + 4 * RATIO, RATIO)
    filtered = jnp.einsum(
        "iy,czyx->czix", yweights, along, preferred_element_type=jnp.float32
    ).astype(jnp.bfloat16)
    ybands = coarse_rows // BY
    xbands = coarse_cols // BX
    count = depth * ybands * xbands
    blocks = filtered.reshape(components, depth, ybands, BY, xbands, BX).transpose(1, 2, 4, 0, 3, 5)
    blocks = blocks.reshape(count, BLKV)
    owners = block_owner.reshape(count)
    slots = block_slot.reshape(count)
    owners_total = lax.axis_size("row")
    every_state, every_rate = (
        lax.all_gather(eddy_state, "row", axis=1, tiled=True),
        lax.all_gather(eddy_rate, "row", axis=1, tiled=True),
    )
    chosen = owners * S + slots
    lookup = (chosen[:, None] == jnp.arange(owners_total * S, dtype=jnp.int32)[None, :]).astype(
        jnp.bfloat16
    )
    state = jnp.dot(lookup, every_state[0], preferred_element_type=jnp.float32)
    rates = jnp.dot(lookup, every_rate[0][:, None], preferred_element_type=jnp.float32)[:, 0]
    forcing_blocks = (rates[:, None] * (state - blocks.astype(jnp.float32))).astype(jnp.bfloat16)
    coarse = forcing_blocks.reshape(depth, ybands, xbands, components, BY, BX).transpose(
        3, 0, 1, 4, 2, 5
    )
    coarse = coarse.reshape(components, depth, coarse_rows, coarse_cols).astype(jnp.float32)
    forcing = jnp.repeat(jnp.repeat(coarse, RATIO, axis=2), RATIO, axis=3)
    speed = velocity.astype(jnp.float32)
    spin = vorticity.astype(jnp.float32)
    cross = jnp.stack(
        [
            speed[1] * spin[2] - speed[2] * spin[1],
            speed[2] * spin[0] - speed[0] * spin[2],
            speed[0] * spin[1] - speed[1] * spin[0],
        ],
        axis=0,
    )
    section = (speed + section_step * (cross + forcing)).astype(jnp.bfloat16)
    xtable = x_table(points, KXM)
    spectrum = jnp.einsum(
        "kyn,nm->kmy",
        section.reshape(components * depth, rows, points),
        xtable,
        preferred_element_type=jnp.float32,
    ).astype(jnp.bfloat16)
    ordered = along_y(lax.all_to_all(spectrum, "row", split_axis=1, concat_axis=2, tiled=True))
    ordered = ordered.reshape(components, depth, KYM, -1)
    inverse = vertical_inverse(depth * lax.axis_size("col")).astype(jnp.bfloat16)
    mode_rows = KYM // lax.axis_size("col")
    mode_cols = ordered.shape[3] // 2
    x_wave = lax.axis_index("row") * mode_cols + jnp.arange(mode_cols, dtype=jnp.int32)
    y_wave = lax.axis_index("col") * mode_rows + jnp.arange(mode_rows, dtype=jnp.int32) - KYM // 2
    factor = damping(x_wave, y_wave, NX, NY).reshape(-1)
    piece = lax.all_to_all(ordered, "col", split_axis=2, concat_axis=1, tiled=True)
    items = piece.shape[0]
    flat = piece.reshape(items, piece.shape[1], -1)
    mixed = jnp.einsum("wz,kzl->kwl", inverse, flat, preferred_element_type=jnp.float32)
    return mixed * factor[None, None, :]


MESH = pl.DeviceIdType.MESH
F32 = jnp.float32
BF16 = jnp.bfloat16
YB = 256
NT = (((1,), (1,)), ((), ()))


def fits(rows, points, n_row, n_col):
    mode_cols, mode_rows = KXM // n_row, KYM // n_col
    return (
        n_row == 4
        and rows % YB == 0
        and points % 1024 == 0
        and points >= 2048
        and mode_cols % 16 == 0
        and (2 * mode_cols) % 128 == 64
        and mode_rows % 32 == 0
        and n_col == 8
    )


def x_tables_t(points, kept, n_row):
    per = kept // n_row
    row = np.arange(2 * kept)
    wave = row // (2 * per) * per + row % per
    imag = row // per % 2
    phase = (wave[:, None] * np.arange(points)[None, :]) % points * (2.0 * math.pi / points)
    value = np.where(imag[:, None] == 0, np.cos(phase), -np.sin(phase)) / math.sqrt(points)
    fine = value.astype(BF16)
    coarse = section_step * fine.astype(np.float32).reshape(2 * kept, points // RATIO, RATIO).sum(2)
    return fine, coarse.astype(BF16)


def y_tables_t(points, kept, quarter):
    s = np.arange(kept // 4)
    out = []
    for q in range(4):
        wave = 4 * s + q - kept // 2
        phase = (wave[:, None] * np.arange(quarter)[None, :]) % points * (2.0 * math.pi / points)
        out.append(np.concatenate([np.cos(phase), np.sin(phase)], axis=1) / math.sqrt(points))
    return np.stack(out).astype(BF16)


def all_kernel(
    vel, vort, xt, xc, tab, mix, eddy, pace, owner, slot, xw, yw, ytop, ybot, out,
    velv, vortv, coarsev, along, edges, every, state, xtv, xcv, tabv, section, repeated, xsend, xrecv, ysend, yrecv, held, done,
    load_sem, es_sem, er_sem, ss_sem, sr_sem, xs_sem, xr_sem, ys_sem, yr_sem, out_sem,
):
    me, mc = lax.axis_index("row"), lax.axis_index("col")
    n_row, n_col = 4, yrecv.shape[1]
    _, rows, points = velv.shape
    width = xsend.shape[2]
    barrier = pltpu.get_barrier_semaphore()
    for d in range(1, n_row):
        pl.semaphore_signal(
            barrier, inc=1, device_id={"row": lax.rem(me + d, n_row)}, device_id_type=MESH
        )
    for d in range(1, n_col):
        pl.semaphore_signal(
            barrier, inc=1, device_id={"col": lax.rem(mc + d, n_col)}, device_id_type=MESH
        )
    loads = []
    for src, dst in (
        (vel, velv), (vort, vortv), (xt, xtv), (xc, xcv), (tab, tabv),
    ):
        loads.append(pltpu.make_async_copy(src, dst, load_sem.at[len(loads)]))
        loads[-1].start()
    for v in range(3 * BY):
        state[v] = eddy[:, v * BX : (v + 1) * BX]
    state[3 * BY] = pace[...]
    pl.semaphore_wait(barrier, n_row + n_col - 2)

    def scopy(d):
        return pltpu.make_async_remote_copy(
            src_ref=state,
            dst_ref=every.at[:, me],
            send_sem=ss_sem.at[d - 1],
            recv_sem=sr_sem.at[me],
            device_id={"row": lax.rem(me + d, n_row)},
            device_id_type=MESH,
        )

    def ecopy(side):
        dest = lax.rem(me + (1 if side == 0 else n_row - 1), n_row)
        lines = slice(rows - 16, rows) if side == 0 else slice(0, 16)
        return pltpu.make_async_remote_copy(
            src_ref=along.at[:, lines, :],
            dst_ref=edges.at[side],
            send_sem=es_sem.at[side],
            recv_sem=er_sem.at[side],
            device_id={"row": dest},
            device_id_type=MESH,
        )

    for d in range(1, n_row):
        scopy(d).start()
    loads[0].wait()
    cells = points // RATIO

    def filter_x(comp, carry):
        for h in range(cells // 256):
            low, high = 256 * RATIO * h - 128, 256 * RATIO * h + 256 * RATIO + 128
            cuts = [(max(low, 0), min(high, points), max(-low, 0))]
            if low < 0:
                cuts.append((points + low, points, 0))
            if high > points:
                cuts.append((0, high - points, points - low))
            total = 0.0
            for start, stop, at in cuts:
                total += jnp.dot(
                    velv[comp, :, start:stop],
                    xw[at : at + stop - start, :],
                    preferred_element_type=F32,
                )
            along[comp, :, 256 * h : 256 * (h + 1)] = total.astype(BF16)
        return carry

    lax.fori_loop(0, 3, filter_x, 0)
    ecopy(0).start()
    ecopy(1).start()
    every[:, me] = state[...]
    for d in range(1, n_row):
        source = lax.rem(me + d, n_row)
        pltpu.make_async_remote_copy(
            src_ref=state,
            dst_ref=every.at[:, source],
            send_sem=ss_sem.at[d - 1],
            recv_sem=sr_sem.at[source],
            device_id={"row": source},
            device_id_type=MESH,
        ).wait_recv()
    ecopy(0).wait_recv()
    ecopy(1).wait_recv()
    slots = every.shape[1] * every.shape[2]
    lows = rows // RATIO
    sides = xw.shape[1] // 2
    smooth = []
    for comp in range(3):
        total = jnp.dot(yw[...], along[comp], preferred_element_type=F32)
        total += jnp.dot(ytop[...], edges[0, comp], preferred_element_type=F32)
        total += jnp.dot(ybot[...], edges[1, comp], preferred_element_type=F32)
        smooth.append(total.astype(BF16).astype(F32))
    deep = lax.broadcasted_iota(jnp.int32, (lows, BY * slots), 1)
    inner = (lax.broadcasted_iota(jnp.int32, (lows, BY * slots), 0) & (BY - 1)) * slots
    flat = lax.broadcasted_iota(jnp.int32, (lows, slots), 1)
    count = owner.shape[1]
    chosen = jnp.broadcast_to((owner[...] * S + slot[...]).astype(F32), (lows, count))
    block = lax.broadcasted_iota(jnp.int32, (lows, count), 1)
    band = lax.broadcasted_iota(jnp.int32, (lows, count), 0) // BY * (cells // BX)
    for q in range(cells // BX):
        name = jnp.sum(jnp.where(block == band + q, chosen, 0.0), axis=1, keepdims=True)
        name = name.astype(jnp.int32)
        pick = jnp.where(deep == inner + name, 1.0, 0.0).astype(BF16)
        rate = jnp.dot(
            jnp.where(flat == name, 1.0, 0.0).astype(BF16),
            every[3 * BY].reshape(slots, BX),
            preferred_element_type=F32,
        )
        for comp in range(3):
            held_state = jnp.dot(
                pick,
                every[comp * BY : (comp + 1) * BY].reshape(BY * slots, BX),
                preferred_element_type=F32,
            )
            lanes = slice(q * BX, (q + 1) * BX)
            coarsev[comp, :, lanes] = (rate * (held_state - smooth[comp][:, lanes])).astype(BF16)
    loads[1].wait()

    far = me // 2
    order = [3 * (1 - far), 2 - far, 1 + 4 * far - me, me]
    fine = lax.broadcasted_iota(jnp.int32, (rows, rows // RATIO), 0) // RATIO
    cell = lax.broadcasted_iota(jnp.int32, (rows, rows // RATIO), 1)
    spread = jnp.where(fine == cell, 1.0, 0.0).astype(BF16)

    def xcopy(comp, k, dest):
        return pltpu.make_async_remote_copy(
            src_ref=xsend.at[comp, k],
            dst_ref=xrecv.at[comp, me],
            send_sem=xs_sem.at[comp, k],
            recv_sem=xr_sem.at[comp, me],
            device_id={"row": dest},
            device_id_type=MESH,
        )

    def xbody(comp, carry):
        b, c = lax.rem(comp + 1, 3), lax.rem(comp + 2, 3)

        def piece(i, inner):
            lines = pl.ds(pl.multiple_of(i * 16, 16), 16)
            cross = velv[b, lines, :].astype(F32) * vortv[c, lines, :].astype(F32)
            cross = cross - velv[c, lines, :].astype(F32) * vortv[b, lines, :].astype(F32)
            section[lines, :] = (velv[comp, lines, :].astype(F32) + section_step * cross).astype(BF16)
            return inner

        lax.fori_loop(0, rows // 16, piece, 0)
        repeated[...] = jnp.dot(spread, coarsev[comp], preferred_element_type=F32).astype(BF16)

        @pl.when(comp == 0)
        def _():
            loads[2].wait()
            loads[3].wait()

        for k in range(n_row):
            lines = pl.ds(pl.multiple_of(order[k] * width, 16), width)
            total = lax.dot_general(xtv[lines, :], section[...], NT, preferred_element_type=F32)
            total += lax.dot_general(xcv[lines, :], repeated[...], NT, preferred_element_type=F32)
            if k < n_row - 1:
                xsend[comp, k] = total.astype(BF16)
                xcopy(comp, k, order[k]).start()
            else:
                xrecv[comp, me] = total.astype(BF16)
        return carry

    lax.fori_loop(0, 3, xbody, 0)
    loads[4].wait()

    def ycopy(comp, d):
        dest = lax.rem(mc + d, n_col)
        return pltpu.make_async_remote_copy(
            src_ref=ysend.at[comp, dest],
            dst_ref=yrecv.at[comp, mc],
            send_sem=ys_sem.at[comp, d - 1],
            recv_sem=yr_sem.at[comp, mc],
            device_id={"col": dest},
            device_id_type=MESH,
        )

    def ystage(comp):
        for d in range(1, n_row):
            source = lax.rem(me + d, n_row)
            pltpu.make_async_remote_copy(
                src_ref=xsend.at[comp, 0],
                dst_ref=xrecv.at[comp, source],
                send_sem=xs_sem.at[comp, 0],
                recv_sem=xr_sem.at[comp, source],
                device_id={"row": source},
                device_id_type=MESH,
            ).wait_recv()
        half = width // 2
        a = [xrecv[comp, r, :half, :].astype(F32) for r in range(4)]
        b = [xrecv[comp, r, half:, :].astype(F32) for r in range(4)]
        a02, a13, b02, b13 = a[0] + a[2], a[1] + a[3], b[0] + b[2], b[1] + b[3]
        d02, d13, e02, e13 = a[0] - a[2], a[1] - a[3], b[0] - b[2], b[1] - b[3]
        real = [a02 + a13, d02 + e13, a02 - a13, d02 - e13]
        imag = [b02 + b13, e02 - d13, b02 - b13, e02 + d13]
        results = []
        for q in range(4):
            re, im = real[q].astype(BF16), imag[q].astype(BF16)
            turned = jnp.concatenate(
                [jnp.concatenate([re, im], axis=0), jnp.concatenate([im, -re], axis=0)], axis=1
            )
            results.append(lax.dot_general(tabv[q], turned, NT, preferred_element_type=F32))
        part = ysend.shape[2] // 4
        for d in range(n_col):
            ysend[comp, d] = jnp.concatenate(
                [results[q][d * part : (d + 1) * part] for q in range(4)], axis=0
            ).astype(BF16)
        for d in range(1, n_col):
            ycopy(comp, d).start()
        yrecv[comp, mc] = ysend[comp, mc]

    def zstage(comp):
        for d in range(1, n_col):
            source = lax.rem(mc + d, n_col)
            pltpu.make_async_remote_copy(
                src_ref=ysend.at[comp, source],
                dst_ref=yrecv.at[comp, source],
                send_sem=ys_sem.at[comp, d - 1],
                recv_sem=yr_sem.at[comp, source],
                device_id={"col": source},
                device_id_type=MESH,
            ).wait_recv()
        lines, planes, _ = held.shape
        part = lines // 4
        for blk in range(lines // 16):
            cut = slice(blk * 16, (blk + 1) * 16)
            group = yrecv[comp, :, cut, :].reshape(planes * 16, width)
            mixed = jnp.dot(mix[...], group, preferred_element_type=F32)
            held[cut] = mixed.reshape(16, planes, width)

        def body(s, carry):
            for pair in range(2):
                left = held[2 * pair * part + s]
                right = held[(2 * pair + 1) * part + s]
                lanes = pl.ds(pl.multiple_of((2 * s + pair) * 2 * width, 128), 2 * width)
                done[comp, :, lanes] = jnp.concatenate([left, right], axis=1)
            return carry

        lax.fori_loop(0, part, body, 0, unroll=4)
        pltpu.make_async_copy(done.at[comp], out.at[comp], out_sem.at[comp]).start()

    ystage(0)
    ystage(1)
    zstage(0)
    ystage(2)
    zstage(1)
    zstage(2)
    for d in range(1, n_row):
        scopy(d).wait_send()
    ecopy(0).wait_send()
    ecopy(1).wait_send()
    for comp in range(3):
        pltpu.make_async_copy(done.at[comp], out.at[comp], out_sem.at[comp]).wait()
        for k in range(n_row - 1):
            xcopy(comp, k, order[k]).wait_send()
        for d in range(1, n_col):
            ycopy(comp, d).wait_send()


def all_stages(vel, vort, xt, xc, tab, mix, small, n_row, n_col):
    _, rows, points = vel.shape
    cells = points // RATIO
    state = (3 * BY + 1, small[0].shape[0], BX)
    width = xt.shape[0] // n_row
    lines = 4 * tab.shape[1] // n_col
    anywhere = pl.BlockSpec(memory_space=pl.ANY)
    dma = pltpu.SemaphoreType.DMA
    return pl.pallas_call(
        all_kernel,
        out_shape=jax.ShapeDtypeStruct((3, n_col, lines * width), F32),
        in_specs=[anywhere] * 5 + [pl.BlockSpec(memory_space=pltpu.VMEM)] * (1 + len(small)),
        out_specs=anywhere,
        scratch_shapes=[
            pltpu.VMEM(vel.shape, BF16),
            pltpu.VMEM(vort.shape, BF16),
            pltpu.VMEM((3, rows // RATIO, cells), BF16),
            pltpu.VMEM((3, rows, cells), BF16),
            pltpu.VMEM((2, 3, 16, cells), BF16),
            pltpu.VMEM((state[0], n_row, state[1], state[2]), BF16),
            pltpu.VMEM(state, BF16),
            pltpu.VMEM(xt.shape, BF16),
            pltpu.VMEM(xc.shape, BF16),
            pltpu.VMEM(tab.shape, BF16),
            pltpu.VMEM((rows, points), BF16),
            pltpu.VMEM((rows, points // RATIO), BF16),
            pltpu.VMEM((3, n_row, width, rows), BF16),
            pltpu.VMEM((3, n_row, width, rows), BF16),
            pltpu.VMEM((3, n_col, lines, width), BF16),
            pltpu.VMEM((3, n_col, lines, width), BF16),
            pltpu.VMEM((lines, n_col, width), F32),
            pltpu.VMEM((3, n_col, lines * width), F32),
            dma((5,)),
            dma((2,)),
            dma((2,)),
            dma((n_row,)),
            dma((n_row,)),
            dma((3, n_row)),
            dma((3, n_row)),
            dma((3, n_col)),
            dma((3, n_col)),
            dma((3,)),
        ],
        compiler_params=pltpu.CompilerParams(
            collective_id=0, has_side_effects=True, vmem_limit_bytes=60 * 2**20
        ),
        name="all_stages",
    )(vel, vort, xt, xc, tab, mix, *small)


def filter_tables(rows):
    taps = np.arange(5 * RATIO) - 2.0 * RATIO - (RATIO - 1) / 2.0
    value = np.exp(-taps * taps / (8.0 * RATIO * RATIO))
    value = value / value.sum()

    def weights(offset):
        inside = (offset >= 0) & (offset < 5 * RATIO)
        return np.where(inside, value[np.clip(offset, 0, 5 * RATIO - 1)], 0.0).astype(BF16)

    fine = np.arange(256 * RATIO + 256)[:, None] - 128
    xw = weights(fine - RATIO * np.arange(256)[None, :] + 2 * RATIO)
    cell = RATIO * np.arange(rows // RATIO)[:, None] - 2 * RATIO
    yw = weights(np.arange(rows)[None, :] - cell)
    edge = np.arange(16)[None, :]
    return xw, yw, weights(edge - 16 - cell), weights(edge + rows - cell)


def vertical_inverse_np(planes):
    index = np.arange(planes)
    ends = (index == 0) | (index == planes - 1)
    matrix = np.diag(np.where(ends, 1.0 + vertical_step, 1.0 + 2.0 * vertical_step))
    for i in range(planes - 1):
        matrix[i, i + 1] = matrix[i + 1, i] = -vertical_step
    return np.linalg.inv(matrix).astype(np.float32)


def per_device(velocity, vorticity, eddy_state, eddy_rate, block_owner, block_slot):
    components, depth, rows, points = velocity.shape
    n_row, n_col = lax.axis_size("row"), lax.axis_size("col")
    if depth != 1 or not fits(rows, points, n_row, n_col):
        return generic_device(velocity, vorticity, eddy_state, eddy_rate, block_owner, block_slot)
    held = eddy_state.shape[1]
    small = [
        eddy_state[0],
        jnp.broadcast_to(eddy_rate[0][:, None], (held, BX)),
        block_owner.reshape(1, -1),
        block_slot.reshape(1, -1),
    ]
    small += [jnp.asarray(t) for t in filter_tables(rows)]
    vel = velocity.reshape(components, rows, points)
    vort = vorticity.reshape(components, rows, points)
    xt, xc = (jnp.asarray(t) for t in x_tables_t(points, KXM, n_row))
    tab = jnp.asarray(y_tables_t(rows * n_row, KYM, rows))
    mix = jnp.asarray(
        np.einsum("vz,ts->tvzs", vertical_inverse_np(n_col), np.eye(16))
        .reshape(16 * n_col, n_col * 16)
        .astype(BF16)
    )
    mode_rows = KYM // n_col
    mode_cols = KXM // n_row
    x_wave = lax.axis_index("row") * mode_cols + jnp.arange(mode_cols, dtype=jnp.int32)
    y_wave = lax.axis_index("col") * mode_rows + jnp.arange(mode_rows, dtype=jnp.int32) - KYM // 2
    factor = damping(x_wave, y_wave, NX, NY).reshape(-1)
    mixed = all_stages(vel, vort, xt, xc, tab, mix, small, n_row, n_col)
    return mixed * factor[None, None, :]


def solution(mesh):
    return jax.shard_map(
        per_device,
        mesh=mesh,
        in_specs=(
            P(None, "col", "row", None),
            P(None, "col", "row", None),
            P("col", "row", None),
            P("col", "row"),
            P("col", "row", None, None),
            P("col", "row", None),
        ),
        out_specs=P(None, None, ("row", "col")),
        check_vma=False,
    )
```

profile of v0, /device:TPU:13, one launch (start us, length us, event | category | flops | bytes accessed | tf_op | source)
XLA Modules:
  0.0 129.9 jit_solution(3067753727832622910)
XLA Ops:
  0.0 1.3 %broadcast_in_dim.7.pace = bf16[16,128]{1,0:T(8,128)(2,1)} broadcast(bf16[16]{0:T(256)(128)(2,1)} %bitcast.11), dimensions={0} | broadcast | bytes 4128 | tf_op jit(solution)/shard_map/broadcast_in_dim | solution.py:589
  1.3 0.1 multiply_exponential_fusion
  1.4 0.1 broadcast_in_dim.8
  1.6 0.4 mul.65
  2.0 123.0 %all_stages.1 = f32[3,8,51200]{2,1,0:T(8,128)} custom-call(bf16[3,512,2048]{2,1,0:T(8,128)(2,1)} %bitcast.6, bf16[3,512,2048]{2,1,0:T(8,128)(2,1)} %bitcast.7, bf16[1280,2048]{1,0:T(8,128)(2,1)} %constant.37.clone.xt, bf16[1280,512]{1,0:T(8,128)(2,1)} %constant.38.clone.xc, bf16[4,320,1024]{2,1,0:T(8,128)(2,1)} %constant.39.clone.tab, ...), custom_call_target="tpu_custom_call" | custom-call | tf_op jit(solution)/shard_map/all_stages/pallas_call | solution.py:513
  124.9 5.0 %broadcast_multiply_fusion = f32[3,8,51200]{2,1,0:T(8,128)} fusion(f32[3,8,51200]{2,1,0:T(8,128)} %all_stages.1, f32[51200]{0:T(1024)S(1)} %mul.65), kind=kLoop, calls=%fused_computation | loop fusion | flops 1228800 | bytes 10035200 | tf_op jit(solution)/shard_map/mul | solution.py:609
  (1 shorter events, 0.0 us)
where the time goes:
time: 130 us
  Pallas kernels  123 us (95%)
  other arithmetic  5.12 us (4%)
  local copies, waits for them, and re-layouts  1.84 us (1%)
    pallas_call x1, Pallas kernels, all_stages(): pl.pallas_call(all_kernel, out_shape=jax.ShapeDtypeStruct((3, n_col, line...  123 us
    mul x1, other arithmetic, per_device(): return mixed * factor[None, None, :]  5.01 us

commit v1 on v0

v1 whole, which is shorter than its diff:
```python
import math

import jax
import jax.numpy as jnp
import numpy as np
from jax import lax
from jax.experimental import pallas as pl
from jax.experimental.pallas import tpu as pltpu
from jax.sharding import PartitionSpec as P

NX = 2048
NY = 2048
KXM = 640
KYM = 1280
RATIO = 4
BY = 8
BX = 128
S = 16
BLKV = 3072


section_step = 0.5
viscous_step = 0.15
vertical_step = 0.5


def padded_2(cells, sides, width):
    for axis, dim in sides:
        count = lax.axis_size(axis)
        head = lax.slice_in_dim(cells, 0, width, axis=dim)
        tail = lax.slice_in_dim(cells, cells.shape[dim] - width, cells.shape[dim], axis=dim)
        cells = jnp.concatenate(
            [
                lax.ppermute(tail, axis, [(i, (i + 1) % count) for i in range(count)]),
                cells,
                lax.ppermute(head, axis, [((i + 1) % count, i) for i in range(count)]),
            ],
            axis=dim,
        )
    return cells


def gauss_value(position, ratio):
    spread = 4.0 * ratio * ratio
    taps = jnp.arange(5 * ratio).astype(jnp.float32)
    shifted = taps - 2.0 * ratio - (ratio - 1) / 2.0
    total = jnp.sum(jnp.exp(-shifted * shifted / (2.0 * spread)))
    moved = position - 2.0 * ratio - (ratio - 1) / 2.0
    return jnp.exp(-moved * moved / (2.0 * spread)) / total


def x_weights(points, coarse, ratio):
    fine = jnp.arange(points, dtype=jnp.int32)[:, None]
    cells = jnp.arange(coarse, dtype=jnp.int32)[None, :]
    offset = jnp.mod(fine - ratio * cells + 2 * ratio, points)
    value = gauss_value(offset.astype(jnp.float32), ratio)
    return jnp.where(offset < 5 * ratio, value, 0.0).astype(jnp.bfloat16)


def y_weights(coarse, padded, ratio):
    cells = jnp.arange(coarse, dtype=jnp.int32)[:, None]
    fine = jnp.arange(padded, dtype=jnp.int32)[None, :]
    offset = fine - ratio * cells
    value = gauss_value(offset.astype(jnp.float32), ratio)
    return jnp.where((offset >= 0) & (offset < 5 * ratio), value, 0.0).astype(jnp.bfloat16)


def x_table(points, kept):
    fine = jnp.arange(points, dtype=jnp.int32)[:, None]
    column = jnp.arange(2 * kept, dtype=jnp.int32)[None, :]
    phase = jnp.mod(column // 2 * fine, points).astype(jnp.float32) * (2.0 * math.pi / points)
    value = jnp.where(column % 2 == 0, jnp.cos(phase), -jnp.sin(phase))
    return (value / math.sqrt(points)).astype(jnp.bfloat16)


def y_tables(points, kept, first, count):
    fine = jnp.arange(points, dtype=jnp.int32)[:, None]
    wave = jnp.arange(count, dtype=jnp.int32)[None, :] + (first - kept // 2)
    phase = jnp.mod(wave * fine, points).astype(jnp.float32) * (2.0 * math.pi / points)
    scale = 1.0 / math.sqrt(points)
    return (
        (jnp.cos(phase) * scale).astype(jnp.bfloat16),
        (jnp.sin(phase) * scale).astype(jnp.bfloat16),
    )


def vertical_inverse(planes):
    index = jnp.arange(planes)
    ends = (index == 0) | (index == planes - 1)
    diagonal = jnp.where(ends, 1.0 + vertical_step, 1.0 + 2.0 * vertical_step).astype(jnp.float32)
    lower = jnp.where(index == 0, 0.0, -vertical_step).astype(jnp.float32)
    upper = jnp.where(index == planes - 1, 0.0, -vertical_step).astype(jnp.float32)
    return lax.linalg.tridiagonal_solve(lower, diagonal, upper, jnp.eye(planes, dtype=jnp.float32))


def damping(x_wave, y_wave, points_x, points_y):
    angle_x = x_wave.astype(jnp.float32) * (2.0 * math.pi / points_x)
    angle_y = y_wave.astype(jnp.float32) * (2.0 * math.pi / points_y)
    total = (
        angle_y[:, None, None] * angle_y[:, None, None]
        + angle_x[None, None, :] * angle_x[None, None, :]
    )
    return jnp.broadcast_to(jnp.exp(-viscous_step * total), (y_wave.shape[0], 2, x_wave.shape[0]))


def along_y(piece):
    items, width, length = piece.shape
    half = width // 2
    split = piece.reshape(items, half, 2, length)
    real_in = split[:, :, 0, :]
    imag_in = split[:, :, 1, :]
    block = 256
    outputs = []
    for first in range(0, KYM, block):
        cosine, sine = y_tables(length, KYM, first, block)
        real_out = jnp.einsum(
            "kin,nj->kji", real_in, cosine, preferred_element_type=jnp.float32
        ) + jnp.einsum("kin,nj->kji", imag_in, sine, preferred_element_type=jnp.float32)
        imag_out = jnp.einsum(
            "kin,nj->kji", imag_in, cosine, preferred_element_type=jnp.float32
        ) - jnp.einsum("kin,nj->kji", real_in, sine, preferred_element_type=jnp.float32)
        outputs.append(jnp.concatenate([real_out, imag_out], axis=2))
    return jnp.concatenate(outputs, axis=1).astype(jnp.bfloat16)


def generic_device(velocity, vorticity, eddy_state, eddy_rate, block_owner, block_slot):
    components, depth, rows, points = velocity.shape
    coarse_rows = rows // RATIO
    coarse_cols = points // RATIO
    xweights = x_weights(points, coarse_cols, RATIO)
    local = jnp.einsum(
        "czyn,nx->czyx", velocity, xweights, preferred_element_type=jnp.float32
    ).astype(jnp.bfloat16)
    along = padded_2(local, (("row", 2),), 2 * RATIO)
    yweights = y_weights(coarse_rows, rows + 4 * RATIO, RATIO)
    filtered = jnp.einsum(
        "iy,czyx->czix", yweights, along, preferred_element_type=jnp.float32
    ).astype(jnp.bfloat16)
    ybands = coarse_rows // BY
    xbands = coarse_cols // BX
    count = depth * ybands * xbands
    blocks = filtered.reshape(components, depth, ybands, BY, xbands, BX).transpose(1, 2, 4, 0, 3, 5)
    blocks = blocks.reshape(count, BLKV)
    owners = block_owner.reshape(count)
    slots = block_slot.reshape(count)
    owners_total = lax.axis_size("row")
    every_state, every_rate = (
        lax.all_gather(eddy_state, "row", axis=1, tiled=True),
        lax.all_gather(eddy_rate, "row", axis=1, tiled=True),
    )
    chosen = owners * S + slots
    lookup = (chosen[:, None] == jnp.arange(owners_total * S, dtype=jnp.int32)[None, :]).astype(
        jnp.bfloat16
    )
    state = jnp.dot(lookup, every_state[0], preferred_element_type=jnp.float32)
    rates = jnp.dot(lookup, every_rate[0][:, None], preferred_element_type=jnp.float32)[:, 0]
    forcing_blocks = (rates[:, None] * (state - blocks.astype(jnp.float32))).astype(jnp.bfloat16)
    coarse = forcing_blocks.reshape(depth, ybands, xbands, components, BY, BX).transpose(
        3, 0, 1, 4, 2, 5
    )
    coarse = coarse.reshape(components, depth, coarse_rows, coarse_cols).astype(jnp.float32)
    forcing = jnp.repeat(jnp.repeat(coarse, RATIO, axis=2), RATIO, axis=3)
    speed = velocity.astype(jnp.float32)
    spin = vorticity.astype(jnp.float32)
    cross = jnp.stack(
        [
            speed[1] * spin[2] - speed[2] * spin[1],
            speed[2] * spin[0] - speed[0] * spin[2],
            speed[0] * spin[1] - speed[1] * spin[0],
        ],
        axis=0,
    )
    section = (speed + section_step * (cross + forcing)).astype(jnp.bfloat16)
    xtable = x_table(points, KXM)
    spectrum = jnp.einsum(
        "kyn,nm->kmy",
        section.reshape(components * depth, rows, points),
        xtable,
        preferred_element_type=jnp.float32,
    ).astype(jnp.bfloat16)
    ordered = along_y(lax.all_to_all(spectrum, "row", split_axis=1, concat_axis=2, tiled=True))
    ordered = ordered.reshape(components, depth, KYM, -1)
    inverse = vertical_inverse(depth * lax.axis_size("col")).astype(jnp.bfloat16)
    mode_rows = KYM // lax.axis_size("col")
    mode_cols = ordered.shape[3] // 2
    x_wave = lax.axis_index("row") * mode_cols + jnp.arange(mode_cols, dtype=jnp.int32)
    y_wave = lax.axis_index("col") * mode_rows + jnp.arange(mode_rows, dtype=jnp.int32) - KYM // 2
    factor = damping(x_wave, y_wave, NX, NY).reshape(-1)
    piece = lax.all_to_all(ordered, "col", split_axis=2, concat_axis=1, tiled=True)
    items = piece.shape[0]
    flat = piece.reshape(items, piece.shape[1], -1)
    mixed = jnp.einsum("wz,kzl->kwl", inverse, flat, preferred_element_type=jnp.float32)
    return mixed * factor[None, None, :]


MESH = pl.DeviceIdType.MESH
F32 = jnp.float32
BF16 = jnp.bfloat16
LANES = 128
HALF = LANES // 2
MARGIN = 32


def fits(rows, points, n_row, n_col):
    mode_cols, mode_rows = KXM // n_row, KYM // n_col
    return (
        n_row == 4
        and n_col == 8
        and rows % 256 == 0
        and points % 1024 == 0
        and points >= 2048
        and mode_cols // HALF == 2
        and mode_cols % HALF == HALF // 2
        and mode_rows % 32 == 0
        and KYM % n_row == 0
        and (KYM // n_row) % 32 == 0
        and KYM // n_row + MARGIN <= rows
    )


def band_basis(rows, points, kept):
    n = np.arange(rows)
    step = np.arange(1, rows)
    off = np.sin(np.pi * step / points) * np.sin(np.pi * (rows - step) / points)
    main = -np.cos(2.0 * np.pi * (n - (rows - 1) / 2.0) / points)
    main = main * np.cos(np.pi * (kept + 1) / points)
    _, vectors = np.linalg.eigh(np.diag(main) + np.diag(off, 1) + np.diag(off, -1))
    basis = vectors[:, ::-1][:, : kept * rows // points + MARGIN]
    side = np.cos(1.0 + 0.7 * n + 0.003 * n * n) @ basis
    return basis * np.where(side < 0, -1.0, 1.0)[None, :]


def x_table_lanes(points, kept, n_row):
    per = kept // n_row
    wave, imag = [], []
    for first, size, lead in ((0, HALF, True), (2 * HALF, per - 2 * HALF, False)):
        for d in range(n_row):
            for ch in range(2 if lead else 1):
                for p in range(2):
                    wave.append(d * per + first + ch * size + np.arange(size))
                    imag.append(np.full(size, p))
    wave, imag = np.concatenate(wave), np.concatenate(imag)
    phase = (np.arange(points)[:, None] * wave[None, :]) % points * (2.0 * math.pi / points)
    value = np.where(imag[None, :] == 0, np.cos(phase), -np.sin(phase)) / math.sqrt(points)
    fine = value.astype(BF16)
    coarse = fine.astype(np.float32).reshape(points // RATIO, RATIO, 2 * kept).sum(1)
    return np.concatenate([fine, (section_step * coarse).astype(BF16)], axis=0)


def y_tables_b(points, kept, basis):
    n = np.arange(basis.shape[0])
    out = []
    for q in range(4):
        wave = 4 * np.arange(kept // 4) + q - kept // 2
        phase = (wave[:, None] * n[None, :]) % points * (2.0 * math.pi / points)
        both = [np.cos(phase) @ basis, np.sin(phase) @ basis]
        out.append(np.concatenate(both, axis=1) / math.sqrt(points))
    return np.stack(out).astype(BF16)


def all_kernel(
    vel, vort, xw, ut, uc, xt, tab, mix, yw, ytop, ybot, eddy, rate, owner, slot, out,
    velv, vortv, xwv, utv, ucv, xtv, tabv, mixv, ywv, ytopv, ybotv,
    along, edges, every, state, picks, flats, coarse, section, projv,
    xsc, xsb, xrc, xrb, ysc, ysb, yrc, yrb, heldc, heldb, fac,
    load_sem, es_sem, er_sem, ss_sem, sr_sem, xs_sem, xr_sem, ys_sem, yr_sem,
):
    me, mc = lax.axis_index("row"), lax.axis_index("col")
    n_row, n_col = xrc.shape[2], yrc.shape[2]
    _, rows, points = velv.shape
    rank = utv.shape[0]
    fold = rank // 2
    cells, lows = points // RATIO, rows // RATIO
    owned = state.shape[2]
    slots = n_row * owned
    barrier = pltpu.get_barrier_semaphore()
    for d in range(1, n_row):
        pl.semaphore_signal(
            barrier, inc=1, device_id={"row": lax.rem(me + d, n_row)}, device_id_type=MESH
        )
    for d in range(1, n_col):
        pl.semaphore_signal(
            barrier, inc=1, device_id={"col": lax.rem(mc + d, n_col)}, device_id_type=MESH
        )
    pairs = [(xw, xwv)] + [(vel.at[c], velv.at[c]) for c in range(3)]
    pairs += [(yw, ywv), (ytop, ytopv), (ybot, ybotv)]
    pairs += [(vort.at[c], vortv.at[c]) for c in (1, 2, 0)]
    pairs += [(ut, utv), (uc, ucv), (xt, xtv), (mix, mixv), (tab, tabv)]
    loads = [pltpu.make_async_copy(a, b, load_sem.at[i]) for i, (a, b) in enumerate(pairs)]
    for load in loads:
        load.start()

    def filter_x(comp):
        for h in range(cells // 256):
            low, high = 256 * RATIO * h - 128, 256 * RATIO * h + 256 * RATIO + 128
            cuts = [(max(low, 0), min(high, points), max(-low, 0))]
            if low < 0:
                cuts.append((points + low, points, 0))
            if high > points:
                cuts.append((0, high - points, points - low))
            total = 0.0
            for start, stop, at in cuts:
                total += jnp.dot(
                    velv[comp, :, start:stop],
                    xwv[at : at + stop - start, :],
                    preferred_element_type=F32,
                )
            along[comp, :, 256 * h : 256 * (h + 1)] = total.astype(BF16)

    def scopy(comp, d):
        return pltpu.make_async_remote_copy(
            src_ref=state.at[comp],
            dst_ref=every.at[comp, :, me],
            send_sem=ss_sem.at[comp, d - 1],
            recv_sem=sr_sem.at[comp, me],
            device_id={"row": lax.rem(me + d, n_row)},
            device_id_type=MESH,
        )

    def ecopy(comp, side):
        dest = lax.rem(me + (1 if side == 0 else n_row - 1), n_row)
        lines = slice(rows - 16, rows) if side == 0 else slice(0, 16)
        return pltpu.make_async_remote_copy(
            src_ref=along.at[comp, lines, :],
            dst_ref=edges.at[side, comp],
            send_sem=es_sem.at[comp, side],
            recv_sem=er_sem.at[comp, side],
            device_id={"row": dest},
            device_id_type=MESH,
        )

    line = lax.broadcasted_iota(jnp.int32, (owned, owned), 0)
    lane = lax.broadcasted_iota(jnp.int32, (owned, owned), 1)
    pace = jnp.where(line == lane, jnp.broadcast_to(rate[...].astype(F32), (owned, owned)), 0.0)
    pace = jnp.broadcast_to(jnp.sum(pace, axis=1, keepdims=True), (owned, BX)).astype(BF16)
    for comp in range(3):
        state[comp, 0] = pace
        for v in range(BY):
            at = (comp * BY + v) * BX
            state[comp, 1 + v] = eddy[:, at : at + BX]
    loads[0].wait()
    loads[1].wait()
    filter_x(0)
    pl.semaphore_wait(barrier, n_row + n_col - 2)

    def spread_out(comp):
        ecopy(comp, 0).start()
        ecopy(comp, 1).start()
        for d in range(1, n_row):
            scopy(comp, d).start()
        every[comp, :, me] = state[comp]

    spread_out(0)
    for comp in range(1, 3):
        loads[1 + comp].wait()
        filter_x(comp)
        spread_out(comp)

    deep = lax.broadcasted_iota(jnp.int32, (lows, BY * slots), 1)
    inner = (lax.broadcasted_iota(jnp.int32, (lows, BY * slots), 0) & (BY - 1)) * slots
    flat = lax.broadcasted_iota(jnp.int32, (lows, slots), 1)
    count = owner.shape[1]
    chosen = jnp.broadcast_to((owner[...] * S + slot[...]).astype(F32), (lows, count))
    block = lax.broadcasted_iota(jnp.int32, (lows, count), 1)
    band = lax.broadcasted_iota(jnp.int32, (lows, count), 0) // BY * (cells // BX)
    for q in range(cells // BX):
        name = jnp.sum(jnp.where(block == band + q, chosen, 0.0), axis=1, keepdims=True)
        name = name.astype(jnp.int32)
        picks[q] = jnp.where(deep == inner + name, 1.0, 0.0).astype(BF16)
        flats[q] = jnp.where(flat == name, 1.0, 0.0).astype(BF16)
    for load in loads[4:12]:
        load.wait()

    far = me // 2
    order = [3 * (1 - far), 2 - far, 1 + 4 * far - me, me]

    def ccopy(comp, ch, k):
        return pltpu.make_async_remote_copy(
            src_ref=xsc.at[comp, ch, k],
            dst_ref=xrc.at[comp, ch, me],
            send_sem=xs_sem.at[comp, ch, k],
            recv_sem=xr_sem.at[comp, ch, me],
            device_id={"row": order[k]},
            device_id_type=MESH,
        )

    def bcopy(comp, k):
        return pltpu.make_async_remote_copy(
            src_ref=xsb.at[comp, order[k]],
            dst_ref=xrb.at[comp, me],
            send_sem=xs_sem.at[comp, 2, k],
            recv_sem=xr_sem.at[comp, 2, me],
            device_id={"row": order[k]},
            device_id_type=MESH,
        )

    def force(comp):
        for d in range(1, n_row):
            source = lax.rem(me + d, n_row)
            pltpu.make_async_remote_copy(
                src_ref=state.at[comp],
                dst_ref=every.at[comp, :, source],
                send_sem=ss_sem.at[comp, d - 1],
                recv_sem=sr_sem.at[comp, source],
                device_id={"row": source},
                device_id_type=MESH,
            ).wait_recv()
        ecopy(comp, 0).wait_recv()
        ecopy(comp, 1).wait_recv()
        total = jnp.dot(ywv[...], along[comp], preferred_element_type=F32)
        total += jnp.dot(ytopv[...], edges[0, comp], preferred_element_type=F32)
        total += jnp.dot(ybotv[...], edges[1, comp], preferred_element_type=F32)
        smooth = total.astype(BF16).astype(F32)
        for q in range(cells // BX):
            pace = jnp.dot(
                flats[q], every[comp, 0].reshape(slots, BX), preferred_element_type=F32
            )
            held_state = jnp.dot(
                picks[q],
                every[comp, 1:].reshape(BY * slots, BX),
                preferred_element_type=F32,
            )
            lanes = slice(q * BX, (q + 1) * BX)
            coarse[:, lanes] = (pace * (held_state - smooth[:, lanes])).astype(BF16)
        projv[:, points:] = jnp.dot(
            ucv[...], coarse[...], preferred_element_type=F32
        ).astype(BF16)

    mid = lax.broadcasted_iota(jnp.int32, (fold, LANES), 1) < HALF

    def xbody(comp, carry):
        b, c = lax.rem(comp + 1, 3), lax.rem(comp + 2, 3)

        def piece(i, inner):
            lines = pl.ds(pl.multiple_of(i * 16, 16), 16)
            cross = velv[b, lines, :].astype(F32) * vortv[c, lines, :].astype(F32)
            cross = cross - velv[c, lines, :].astype(F32) * vortv[b, lines, :].astype(F32)
            section[lines, :] = (velv[comp, lines, :].astype(F32) + section_step * cross).astype(BF16)
            return inner

        lax.fori_loop(0, rows // 16, piece, 0)
        for at in range(0, points, 512):
            projv[:, at : at + 512] = jnp.dot(
                utv[...], section[:, at : at + 512], preferred_element_type=F32
            ).astype(BF16)
        force(comp)

        @pl.when(comp == 0)
        def _():
            loads[12].wait()

        for k in range(n_row):
            at = pl.ds(pl.multiple_of(order[k] * 2 * LANES, 2 * LANES), 2 * LANES)
            total = jnp.dot(projv[...], xtv[:, at], preferred_element_type=F32).astype(BF16)
            if k < n_row - 1:
                xsc[comp, 0, k] = total[:, :LANES]
                xsc[comp, 1, k] = total[:, LANES:]
                ccopy(comp, 0, k).start()
            else:
                xrc[comp, 0, me] = total[:, :LANES]
                xrc[comp, 1, me] = total[:, LANES:]
            if k == 1:
                ccopy(comp, 1, 0).start()
                ccopy(comp, 1, 1).start()
            if k == 2:
                ccopy(comp, 1, 2).start()
        first = 2 * n_row * LANES
        total = jnp.dot(projv[...], xtv[:, first:], preferred_element_type=F32)
        for d in range(n_row):
            part = total[:, d // 2 * LANES : (d // 2 + 1) * LANES]
            low, high = part[:fold], part[fold:]
            if d % 2 == 0:
                both = jnp.where(mid, low, pltpu.roll(high, HALF, 1))
            else:
                both = jnp.where(mid, pltpu.roll(low, HALF, 1), high)
            xsb[comp, d] = both.astype(BF16)
        for k in (2, 0, 1):
            bcopy(comp, k).start()
        xrb[comp, me] = xsb[comp, me]
        return carry

    lax.fori_loop(0, 3, xbody, 0)
    loads[13].wait()
    loads[14].wait()

    part = ysc.shape[3] // 4
    wide = fac.shape[1]
    width = wide // 2
    row = lax.broadcasted_iota(jnp.int32, fac.shape, 0)
    lane = lax.broadcasted_iota(jnp.int32, fac.shape, 1)
    right = jnp.where(lane >= width, 1, 0)
    lane = lane - width * right
    lane = lane - width // 2 * jnp.where(lane >= width // 2, 1, 0)
    angle_x = (me * (width // 2) + lane).astype(F32) * (2.0 * math.pi / NX)
    angle_y = (mc * (4 * part) + 2 * row + right - KYM // 2).astype(F32) * (2.0 * math.pi / NY)
    fac[...] = jnp.exp(-viscous_step * (angle_y * angle_y + angle_x * angle_x))

    flips = [6, 7, 4, 5, 2, 3, 1]

    def ycopy(sent, got, comp, ch, i):
        dest = mc ^ flips[i]
        return pltpu.make_async_remote_copy(
            src_ref=sent.at[dest],
            dst_ref=got.at[mc],
            send_sem=ys_sem.at[comp, ch, i],
            recv_sem=yr_sem.at[comp, ch, mc],
            device_id={"col": dest},
            device_id_type=MESH,
        )

    def ywait(sent, got, comp, ch):
        for i in range(n_col - 1):
            source = mc ^ flips[i]
            pltpu.make_async_remote_copy(
                src_ref=sent.at[source],
                dst_ref=got.at[source],
                send_sem=ys_sem.at[comp, ch, i],
                recv_sem=yr_sem.at[comp, ch, source],
                device_id={"col": source},
                device_id_type=MESH,
            ).wait_recv()

    def xwait(sent, got, comp, ch):
        for d in range(1, n_row):
            source = lax.rem(me + d, n_row)
            pltpu.make_async_remote_copy(
                src_ref=sent,
                dst_ref=got.at[source],
                send_sem=xs_sem.at[comp, ch, 0],
                recv_sem=xr_sem.at[comp, ch, source],
                device_id={"row": source},
                device_id_type=MESH,
            ).wait_recv()

    def quarters(z, turn):
        s02, s13, d02, d13 = z[0] + z[2], z[1] + z[3], z[0] - z[2], z[1] - z[3]
        t13 = turn(d13)
        return [s02 + s13, d02 + t13, s02 - s13, d02 - t13]

    def lanes_of(count):
        return lax.broadcasted_iota(jnp.int32, (count, LANES), 1)

    def turn_c(x):
        moved = pltpu.roll(x, HALF, 1)
        return jnp.where(lanes_of(x.shape[0]) < HALF, moved, -moved)

    def turn_b(x):
        ahead, back = pltpu.roll(x, LANES - HALF // 2, 1), pltpu.roll(x, HALF // 2, 1)
        return jnp.where((lanes_of(x.shape[0]) & (HALF // 2)) == 0, ahead, -back)

    def ystage_c(comp, ch):
        got = xrc.at[comp, ch]
        xwait(xsc.at[comp, ch, 0], got, comp, ch)
        mixed = quarters([xrc[comp, ch, r].astype(F32) for r in range(4)], turn_c)
        results = []
        for q in range(4):
            both = jnp.concatenate([mixed[q], turn_c(mixed[q])], axis=0).astype(BF16)
            results.append(jnp.dot(tabv[q], both, preferred_element_type=F32))
        for d in range(n_col):
            ysc[comp, ch, d] = jnp.concatenate(
                [results[q][d * part : (d + 1) * part] for q in range(4)], axis=0
            ).astype(BF16)
        for i in range(n_col - 1):
            ycopy(ysc.at[comp, ch], yrc.at[comp, ch], comp, ch, i).start()
        yrc[comp, ch, mc] = ysc[comp, ch, mc]

    def ystage_b(comp):
        xwait(xsb.at[comp, 0], xrb.at[comp], comp, 2)
        mixed = quarters([xrb[comp, r].astype(F32) for r in range(4)], turn_b)
        results = []
        for q in range(4):
            stack = []
            for x in (mixed[q], turn_b(mixed[q])):
                moved = pltpu.roll(x, HALF, 1)
                stack += [x, moved] if q % 2 == 0 else [moved, x]
            both = jnp.concatenate(stack, axis=0).astype(BF16)
            results.append(jnp.dot(tabv[q], both, preferred_element_type=F32))
        near = lanes_of(results[0].shape[0]) < HALF
        joined = [jnp.where(near, results[2 * p], results[2 * p + 1]) for p in range(2)]
        for d in range(n_col):
            ysb[comp, d] = jnp.concatenate(
                [joined[p][d * part : (d + 1) * part] for p in range(2)], axis=0
            ).astype(BF16)
        for i in range(n_col - 1):
            ycopy(ysb.at[comp], yrb.at[comp], comp, 2, i).start()
        yrb[comp, mc] = ysb[comp, mc]

    def zstage(comp):
        ywait(ysc.at[comp, 0], yrc.at[comp, 0], comp, 0)
        ywait(ysc.at[comp, 1], yrc.at[comp, 1], comp, 1)
        for blk in range(4 * part // 16):
            cut = slice(blk * 16, (blk + 1) * 16)
            group = jnp.concatenate(
                [yrc[comp, ch, :, cut, :].reshape(n_col * 16, LANES) for ch in range(2)], axis=1
            )
            mixed = jnp.dot(mixv[...], group, preferred_element_type=F32)
            heldc[cut] = mixed.reshape(16, n_col, 2 * LANES)
        ywait(ysb.at[comp], yrb.at[comp], comp, 2)
        for blk in range(2 * part // 16):
            cut = slice(blk * 16, (blk + 1) * 16)
            group = yrb[comp, :, cut, :].reshape(n_col * 16, LANES)
            mixed = jnp.dot(mixv[...], group, preferred_element_type=F32)
            heldb[cut] = mixed.reshape(16, n_col, LANES)
        lane = lanes_of(n_col)
        quarter = HALF // 2

        def split(pair):
            low, high = pair[:, :LANES], pair[:, LANES:]
            real = jnp.where(lane < HALF, low, pltpu.roll(high, HALF, 1))
            imag = jnp.where(lane < HALF, pltpu.roll(low, HALF, 1), high)
            return real, imag

        def body(s, carry):
            for p in range(2):
                re_l, im_l = split(heldc[2 * p * part + s])
                re_r, im_r = split(heldc[(2 * p + 1) * part + s])
                rest = heldb[p * part + s]
                im_l, re_r = pltpu.roll(im_l, quarter, 1), pltpu.roll(re_r, HALF, 1)
                im_r = pltpu.roll(im_r, HALF + quarter, 1)
                line = [
                    re_l,
                    jnp.where(lane < quarter, rest, im_l),
                    jnp.where(lane < quarter, im_l, jnp.where(lane < HALF, rest, re_r)),
                    jnp.where(lane < HALF, re_r, jnp.where(lane < HALF + quarter, rest, im_r)),
                    jnp.where(lane < HALF + quarter, im_r, rest),
                ]
                lanes = pl.ds(pl.multiple_of((2 * s + p) * wide, LANES), wide)
                scale = fac[pl.ds(2 * s + p, 1), :]
                out[comp, :, lanes] = jnp.concatenate(line, axis=1) * scale
            return carry

        lax.fori_loop(0, part, body, 0, unroll=4)

    def ybody(comp, carry):
        lax.fori_loop(0, 2, lambda ch, inner: (ystage_c(comp, ch), inner)[1], 0)
        ystage_b(comp)
        zstage(comp)
        return carry

    lax.fori_loop(0, 3, ybody, 0)

    def finish(comp, carry):
        for d in range(1, n_row):
            scopy(comp, d).wait_send()
        ecopy(comp, 0).wait_send()
        ecopy(comp, 1).wait_send()
        for k in range(n_row - 1):
            ccopy(comp, 0, k).wait_send()
            ccopy(comp, 1, k).wait_send()
            bcopy(comp, k).wait_send()
        for i in range(n_col - 1):
            ycopy(ysc.at[comp, 0], yrc.at[comp, 0], comp, 0, i).wait_send()
            ycopy(ysc.at[comp, 1], yrc.at[comp, 1], comp, 1, i).wait_send()
            ycopy(ysb.at[comp], yrb.at[comp], comp, 2, i).wait_send()
        return carry

    lax.fori_loop(0, 3, finish, 0)


def all_stages(big, small, n_row, n_col):
    vel, vort, xw, ut, uc, xt, tab, mix, yw, ytop, ybot = big
    _, rows, points = vel.shape
    cells, lows = points // RATIO, rows // RATIO
    owned = small[0].shape[0]
    rank = ut.shape[0]
    lines = KYM // n_col
    wide = 4 * KXM // n_row
    dma = pltpu.SemaphoreType.DMA
    scratch = [pltpu.VMEM(a.shape, BF16) for a in big]
    scratch += [
        pltpu.VMEM((3, rows, cells), BF16),
        pltpu.VMEM((2, 3, 16, cells), BF16),
        pltpu.VMEM((3, 1 + BY, n_row, owned, BX), BF16),
        pltpu.VMEM((3, 1 + BY, owned, BX), BF16),
        pltpu.VMEM((cells // BX, lows, BY * n_row * owned), BF16),
        pltpu.VMEM((cells // BX, lows, n_row * owned), BF16),
        pltpu.VMEM((lows, cells), BF16),
        pltpu.VMEM((rows, points), BF16),
        pltpu.VMEM((rank, points + cells), BF16),
        pltpu.VMEM((3, 2, n_row - 1, rank, LANES), BF16),
        pltpu.VMEM((3, n_row, rank // 2, LANES), BF16),
        pltpu.VMEM((3, 2, n_row, rank, LANES), BF16),
        pltpu.VMEM((3, n_row, rank // 2, LANES), BF16),
        pltpu.VMEM((3, 2, n_col, lines, LANES), BF16),
        pltpu.VMEM((3, n_col, lines // 2, LANES), BF16),
        pltpu.VMEM((3, 2, n_col, lines, LANES), BF16),
        pltpu.VMEM((3, n_col, lines // 2, LANES), BF16),
        pltpu.VMEM((lines, n_col, 2 * LANES), F32),
        pltpu.VMEM((lines // 2, n_col, LANES), F32),
        pltpu.VMEM((lines // 2, wide), F32),
        dma((len(big) + 4,)),
        dma((3, 2)),
        dma((3, 2)),
        dma((3, n_row)),
        dma((3, n_row)),
        dma((3, 3, n_row)),
        dma((3, 3, n_row)),
        dma((3, 3, n_col)),
        dma((3, 3, n_col)),
    ]
    anywhere = pl.BlockSpec(memory_space=pl.ANY)
    vmem = pl.BlockSpec(memory_space=pltpu.VMEM)
    return pl.pallas_call(
        all_kernel,
        out_shape=pltpu.VMEM((3, n_col, lines * wide // 2), F32),
        in_specs=[anywhere] * len(big) + [vmem] * len(small),
        out_specs=vmem,
        scratch_shapes=scratch,
        compiler_params=pltpu.CompilerParams(
            collective_id=0, has_side_effects=True, vmem_limit_bytes=54 * 2**20
        ),
        name="all_stages",
    )(*big, *small)


def filter_tables(rows):
    taps = np.arange(5 * RATIO) - 2.0 * RATIO - (RATIO - 1) / 2.0
    value = np.exp(-taps * taps / (8.0 * RATIO * RATIO))
    value = value / value.sum()

    def weights(offset):
        inside = (offset >= 0) & (offset < 5 * RATIO)
        return np.where(inside, value[np.clip(offset, 0, 5 * RATIO - 1)], 0.0).astype(BF16)

    fine = np.arange(256 * RATIO + 256)[:, None] - 128
    xw = weights(fine - RATIO * np.arange(256)[None, :] + 2 * RATIO)
    cell = RATIO * np.arange(rows // RATIO)[:, None] - 2 * RATIO
    yw = weights(np.arange(rows)[None, :] - cell)
    edge = np.arange(16)[None, :]
    return xw, yw, weights(edge - 16 - cell), weights(edge + rows - cell)


def vertical_inverse_np(planes):
    index = np.arange(planes)
    ends = (index == 0) | (index == planes - 1)
    matrix = np.diag(np.where(ends, 1.0 + vertical_step, 1.0 + 2.0 * vertical_step))
    for i in range(planes - 1):
        matrix[i, i + 1] = matrix[i + 1, i] = -vertical_step
    return np.linalg.inv(matrix).astype(np.float32)


def per_device(velocity, vorticity, eddy_state, eddy_rate, block_owner, block_slot):
    components, depth, rows, points = velocity.shape
    n_row, n_col = lax.axis_size("row"), lax.axis_size("col")
    if depth != 1 or not fits(rows, points, n_row, n_col):
        return generic_device(velocity, vorticity, eddy_state, eddy_rate, block_owner, block_slot)
    basis = band_basis(rows, rows * n_row, KYM)
    ut = np.ascontiguousarray(basis.T).astype(BF16)
    uc = ut.astype(np.float32).reshape(ut.shape[0], rows // RATIO, RATIO).sum(2).astype(BF16)
    xw, yw, ytop, ybot = filter_tables(rows)
    mix = np.einsum("vz,ts->tvzs", vertical_inverse_np(n_col), np.eye(16))
    mix = mix.reshape(16 * n_col, n_col * 16).astype(BF16)
    xt = x_table_lanes(points, KXM, n_row)
    tab = y_tables_b(rows * n_row, KYM, basis)
    big = [velocity.reshape(components, rows, points), vorticity.reshape(components, rows, points)]
    big += [jnp.asarray(t) for t in (xw, ut, uc, xt, tab, mix, yw, ytop, ybot)]
    small = [
        eddy_state[0],
        eddy_rate,
        block_owner.reshape(1, -1),
        block_slot.reshape(1, -1),
    ]
    return all_stages(big, small, n_row, n_col)


def solution(mesh):
    return jax.shard_map(
        per_device,
        mesh=mesh,
        in_specs=(
            P(None, "col", "row", None),
            P(None, "col", "row", None),
            P("col", "row", None),
            P("col", "row"),
            P("col", "row", None, None),
            P("col", "row", None),
        ),
        out_specs=P(None, None, ("row", "col")),
        check_vma=False,
    )
```

time: 130 us -> 95.6 us (0.74); the launches traced: 130 us -> 93.7 us
  Pallas kernels: 123 us -> 91.5 us
  other arithmetic: 5.12 us -> 0 us
    pallas_call x1, Pallas kernels: 123 us -> 91.5 us  [all_stages(): pl.pallas_call(all_kernel, out_shape=pltpu.VMEM((3, n_col, lines * wide /...]
    mul x2 -> x0, other arithmetic: 5.02 us -> none  [the longest x1 5.01 us: per_device(): return mixed * factor[None, None, :]]
    unnamed x0 -> x1, local copies, waits for them, and re-layouts: none -> 2.25 us
    broadcast_in_dim x2 -> x0, local copies, waits for them, and re-layouts: 1.43 us -> none  [the longest x1 1.32 us: per_device(): jnp.broadcast_to(eddy_rate[0][:, None], (held, BX))]
where the time goes in v1:
time: 95.6 us; the launch traced here: 93.7 us
  Pallas kernels  91.5 us (96%)
  local copies, waits for them, and re-layouts  2.25 us (2%)
    pallas_call x1, Pallas kernels, all_stages(): pl.pallas_call(all_kernel, out_shape=pltpu.VMEM((3, n_col, lines * wide /...  91.5 us
    unnamed x1, local copies, waits for them, and re-layouts  2.25 us

profile of v1, /device:TPU:13, one launch (start us, length us, event | category | flops | bytes accessed | tf_op | source)
XLA Modules:
  0.0 93.7 jit_solution(20149988292581087)
XLA Ops:
  0.0 91.5 %all_stages.1 = f32[3,8,51200]{2,1,0:T(8,128)S(1)} custom-call(bf16[3,512,2048]{2,1,0:T(8,128)(2,1)} %bitcast.5, bf16[3,512,2048]{2,1,0:T(8,128)(2,1)} %bitcast.6, bf16[1280,256]{1,0:T(8,128)(2,1)} %constant.18.clone.xw, bf16[352,512]{1,0:T(8,128)(2,1)} %constant.19.clone.ut, bf16[352,128]{1,0:T(8,128)(2,1)} %constant.20.clone.uc, ...), custom_call_target="tpu_custom_call" | custom-call | tf_op jit(solution)/shard_map/all_stages/pallas_call | solution.py:703
  91.5 2.3 %copy.17 = f32[3,8,51200]{2,1,0:T(8,128)} copy(f32[3,8,51200]{2,1,0:T(8,128)S(1)} %all_stages.1) | data formatting | bytes 9830400
